TPU v7x, 32 devices: a whole 2x2x4 slice. The times are simulated.
32 devices in a mesh: seq: 8 (over y, x, core), head: 4 (over z).
Axes of the slice: x: 2, y: 2, z: 4, core: 2. Of those that a mesh axis runs over, the one named last changes fastest.
Arguments:
- queries: bfloat16 [2, 8, 8, 32, 128], P(None, 'head'), may hold values from -128 to 128
- tree_keys: bfloat16 [2, 8, 32, 128], P(None, 'head'), may hold values from -8 to 8
- tree_values: bfloat16 [2, 8, 32, 128], P(None, 'head'), may hold values from -6 to 6
- cache_keys: bfloat16 [8, 8192, 128], P('head', 'seq'), may hold values from -6 to 6
- cache_values: bfloat16 [8, 8192, 128], P('head', 'seq'), may hold values from -6 to 6
- block_ids: int32 [8, 32], P('head'), may hold values from 0 to 63, as said below
- ancestors: int32 [1, 32, 32], replicated, may hold values from 0 to 1, as said below
- out_weight: bfloat16 [8192, 8192], P('seq', 'head'), may hold values from -0.0625 to 0.0625
Outputs:
- draft_mixed: bfloat16 [32, 1, 8192], P('seq', None, 'head')
- verify_mixed: bfloat16 [32, 1, 8192], P('seq', None, 'head')
Inputs may be any that keep to these rules, and one draw needn't show every extreme that they name: `block_ids`: the 32 block numbers of one pair are distinct, and for every pair one run of 1024 positions (positions s * 1024 to (s + 1) * 1024 - 1 for some s) holds at least half of its 32 blocks, or all 8 blocks of the run where the run has fewer. ancestors[r, n, k] is 1 exactly when k is n or an ancestor of n in request r's tree; node 0 is the root and every other node's parent has a smaller number.
All inputs are finite; a program needn't handle non-finite values.
Results may differ from a plain program's by a relative error of at most 0.009.
Values may be sent and summed in bfloat16 or wider, within the bound.
A program may use at most 64 MiB of HBM per device.

v0:
```python
import jax
import jax.numpy as jnp
from jax import lax
from jax.sharding import PartitionSpec as P

KVH = 8
BLOCK = 128


def cache_partial(query_rows, key_rows, value_rows, chosen_mask, score_scale):
    scores = (
        jnp.einsum("pgnh,plh->pgnl", query_rows, key_rows, preferred_element_type=jnp.float32)
        * score_scale
    )
    if chosen_mask is not None:
        scores = jnp.where(chosen_mask[:, None, None, :], scores, -1e30)
    peaks = jnp.max(scores, axis=-1)
    weights = jnp.exp(scores - peaks[..., None])
    if chosen_mask is not None:
        weights = jnp.where(chosen_mask[:, None, None, :], weights, 0.0)
    totals = jnp.sum(weights, axis=-1)
    summed = jnp.einsum(
        "pgnl,plh->pgnh",
        weights.astype(jnp.bfloat16),
        value_rows,
        preferred_element_type=jnp.float32,
    )
    return (peaks, totals, summed)


def tree_partial(query_rows, tree_key_rows, tree_value_rows, tree_mask, score_scale):
    scores = (
        jnp.einsum("pgnh,pkh->pgnk", query_rows, tree_key_rows, preferred_element_type=jnp.float32)
        * score_scale
    )
    allowed = tree_mask[:, None] > 0
    scores = jnp.where(allowed, scores, -1e30)
    peaks = jnp.max(scores, axis=-1)
    weights = jnp.where(allowed, jnp.exp(scores - peaks[..., None]), 0.0)
    totals = jnp.sum(weights, axis=-1)
    summed = jnp.einsum(
        "pgnk,pkh->pgnh",
        weights.astype(jnp.bfloat16),
        tree_value_rows,
        preferred_element_type=jnp.float32,
    )
    return (peaks, totals, summed)


def combine_two(first_part, second_part):
    peaks = jnp.maximum(first_part[0], second_part[0])
    first_factor = jnp.exp(first_part[0] - peaks)
    second_factor = jnp.exp(second_part[0] - peaks)
    totals = first_part[1] * first_factor + second_part[1] * second_factor
    summed = first_part[2] * first_factor[..., None] + second_part[2] * second_factor[..., None]
    return (peaks, totals, summed)


def combine_over(peaks, totals, summed):
    highest = jnp.max(peaks, axis=0)
    factor = jnp.exp(peaks - highest[None])
    return (highest, jnp.sum(totals * factor, axis=0), jnp.sum(summed * factor[..., None], axis=0))


def finish(cache_part, tree_part):
    peaks, totals, summed = combine_two(cache_part, tree_part)
    result = summed / totals[..., None]
    pair_count, groups, node_count, head_dim = result.shape
    return (
        jnp.transpose(result, (0, 2, 1, 3))
        .reshape(pair_count, node_count, groups * head_dim)
        .astype(jnp.bfloat16)
    )


def local(
    queries, tree_keys, tree_values, cache_keys, cache_values, block_ids, ancestors, out_weight
):
    pair_dev, ctx_dev, head_dim = cache_keys.shape
    groups = queries.shape[2]
    node_count = queries.shape[3]
    requests = ancestors.shape[0]
    score_scale = head_dim ** (-0.5)
    seq_count = lax.axis_size("seq")
    seq_index = lax.axis_index("seq")
    head_index = lax.axis_index("head")
    blocks_dev = ctx_dev // BLOCK
    node_dev = node_count // seq_count
    pair_ids = head_index * pair_dev + jnp.arange(pair_dev, dtype=jnp.int32)
    picker = (pair_ids[:, None] // KVH == jnp.arange(requests, dtype=jnp.int32)[None, :]).astype(
        jnp.int32
    )
    tree_masks = jnp.sum(picker[:, :, None, None] * ancestors[None], axis=1)
    verify_part = cache_partial(queries[1], cache_keys, cache_values, None, score_scale)
    owned_ids = seq_index * blocks_dev + jnp.arange(blocks_dev, dtype=jnp.int32)
    chosen = jnp.any(block_ids[:, :, None] == owned_ids[None, None, :], axis=1)
    chosen_mask = jnp.broadcast_to(chosen[:, :, None], (pair_dev, blocks_dev, BLOCK)).reshape(
        pair_dev, ctx_dev
    )
    draft_part = cache_partial(queries[0], cache_keys, cache_values, chosen_mask, score_scale)
    arrived = (
        lax.all_to_all(draft_part[0][None], "seq", split_axis=3, concat_axis=0, tiled=True),
        lax.all_to_all(draft_part[1][None], "seq", split_axis=3, concat_axis=0, tiled=True),
        lax.all_to_all(draft_part[2][None], "seq", split_axis=3, concat_axis=0, tiled=True),
        lax.all_to_all(verify_part[0][None], "seq", split_axis=3, concat_axis=0, tiled=True),
        lax.all_to_all(verify_part[1][None], "seq", split_axis=3, concat_axis=0, tiled=True),
        lax.all_to_all(verify_part[2][None], "seq", split_axis=3, concat_axis=0, tiled=True),
    )
    draft_cache = combine_over(arrived[0], arrived[1], arrived[2])
    verify_cache = combine_over(arrived[3], arrived[4], arrived[5])
    row_start = seq_index * node_dev
    mask_rows = lax.dynamic_slice_in_dim(tree_masks, row_start, node_dev, 1)
    draft_tree = tree_partial(
        lax.dynamic_slice_in_dim(queries[0], row_start, node_dev, 2),
        tree_keys[0],
        tree_values[0],
        mask_rows,
        score_scale,
    )
    verify_tree = tree_partial(
        lax.dynamic_slice_in_dim(queries[1], row_start, node_dev, 2),
        tree_keys[1],
        tree_values[1],
        mask_rows,
        score_scale,
    )
    draft_all, verify_all = (
        lax.all_gather(finish(draft_cache, draft_tree), "seq", axis=1, tiled=True),
        lax.all_gather(finish(verify_cache, verify_tree), "seq", axis=1, tiled=True),
    )
    gathered = (
        lax.all_gather(draft_all, "head", axis=0, tiled=True),
        lax.all_gather(verify_all, "head", axis=0, tiled=True),
    )
    stacked = jnp.stack(gathered)
    stacked = stacked.reshape(2, requests, KVH, node_count, groups * head_dim)
    stacked = jnp.transpose(stacked, (3, 0, 1, 2, 4)).reshape(
        node_count, 2 * requests, KVH * groups * head_dim
    )
    rows_dev = out_weight.shape[0]
    columns = lax.dynamic_slice_in_dim(stacked, seq_index * rows_dev, rows_dev, 2)
    own_rows = lax.psum_scatter(
        jnp.einsum("nrk,kd->nrd", columns, out_weight, preferred_element_type=jnp.float32),
        "seq",
        scatter_dimension=0,
        tiled=True,
    )
    own_rows = own_rows.reshape(node_dev, 2, requests, own_rows.shape[-1]).astype(jnp.bfloat16)
    return (own_rows[:, 0], own_rows[:, 1])


def solution(mesh):
    in_specs = (
        P(None, "head", None, None, None),
        P(None, "head", None, None),
        P(None, "head", None, None),
        P("head", "seq", None),
        P("head", "seq", None),
        P("head", None),
        P(),
        P("seq", "head"),
    )
    out_specs = (P("seq", None, "head"), P("seq", None, "head"))
    return jax.shard_map(local, mesh=mesh, in_specs=in_specs, out_specs=out_specs, check_vma=False)
```

profile of v0, /device:TPU:0, one launch (start us, length us, event | category | flops | bytes accessed | tf_op | source)
XLA Modules:
  0.0 145.6 jit_solution(11215316324020661436)
XLA Ops:
  0.6 0.0 copy-start
  0.7 0.9 compare_reduce_fusion
  1.6 0.1 broadcast_bitcast_fusion
  1.7 0.0 copy-start.5
  1.7 0.0 copy-done
  1.7 1.5 %fusion.2 = (f32[2,8,32]{2,1,0:T(8,128)S(1)}, f32[2,8,32,1024]{3,2,1,0:T(8,128)S(1)}) fusion(pred[2,1024]{1,0:T(4,128)(4,1)S(1)} %bitcast.216, bf16[2,1024,128]{2,1,0:T(8,128)(2,1)S(1)} %copy-done, bf16[2,2,8,32,128]{4,3,2,1,0:T(8,128)(2,1)} %param.8), kind=kOutput, calls=%fused_computation.6 | convolution fusion | flops 135790080 | bytes 2756608 | tf_op jit(solution)/shard_map/pgnh,plh->pgnl/dot_general | solution.py:12
  3.2 0.0 copy-start.1
  3.2 0.0 copy-done.5
  3.2 1.3 copy-done.1
  4.5 0.6 fusion.5
  5.2 0.7 copy.50
  5.9 5.2 %all-to-all-start.2 = ((f32[1,2,8,32]{2,1,0,3:T(2,128)}), f32[1,2,8,32]{2,1,0,3:T(2,128)}, u32[]{:S(2)}, u32[]{:S(2)}) async-start(f32[1,2,8,32]{2,1,0,3:T(2,128)} %copy.50), calls=%async_computation.2 | async-start | bytes 65536 | tf_op jit(solution)/shard_map/all_to_all | solution.py:103
  11.1 0.0 copy-done.2
  11.1 0.7 fusion.81
  11.8 0.5 multiply_reduce_fusion
  12.3 0.0 copy-done.3
  12.3 3.0 %convolution_bitcast_fusion.1 = f32[1,2,8,32,128]{4,3,2,1,0:T(8,128)} fusion(f32[2,8,32,1024]{3,2,1,0:T(8,128)} %copy-done.1, f32[2,8,32]{2,1,0:T(8,128)S(1)} %get-tuple-element.24, pred[2,1024]{1,0:T(4,128)(4,1)} %bitcast.218, bf16[2,1024,128]{2,1,0:T(8,128)(2,1)S(1)} %copy-done.3), kind=kOutput, calls=%fused_computation.12 | convolution fusion | flops 136839168 | bytes 2887680 | tf_op jit(solution)/shard_map/pgnl,plh->pgnh/dot_general | solution.py:22
  15.3 0.7 constant_dynamic-slice_fusion.2
  16.0 0.1 fusion.67
  16.1 0.8 constant_dynamic-slice_fusion
  16.8 0.6 convolution_bitcast_fusion
  17.4 0.0 copy-start.4
  17.4 0.0 copy-start.10
  17.4 0.2 fusion.83
  17.7 0.2 fusion.82
  17.9 0.0 copy-done.7
  17.9 0.0 copy-start.8
  17.9 0.7 copy.45
  18.6 0.0 all-to-all-done.2
  18.6 4.2 %all-to-all-start.1 = ((f32[1,2,8,32]{2,1,0,3:T(2,128)}), f32[1,2,8,32]{2,1,0,3:T(2,128)S(1)}, u32[]{:S(2)}, u32[]{:S(2)}) async-start(f32[1,2,8,32]{2,1,0,3:T(2,128)} %copy.45), calls=%async_computation.1 | async-start | bytes 65536 | tf_op jit(solution)/shard_map/all_to_all | solution.py:102
  22.8 0.5 fusion.3
  23.3 0.0 copy-start.9
  23.3 0.7 copy.56
  24.0 3.6 %all-to-all-done.1 = f32[1,2,8,32]{2,1,0,3:T(2,128)S(1)} async-done(((f32[1,2,8,32]{2,1,0,3:T(2,128)}), f32[1,2,8,32]{2,1,0,3:T(2,128)S(1)}, u32[]{:S(2)}, u32[]{:S(2)}) %all-to-all-start.1) | async-done | bytes 2080 | tf_op jit(solution)/shard_map/all_to_all | solution.py:102
  27.6 3.3 %all-to-all-start.4 = ((f32[1,2,8,32]{2,1,0,3:T(2,128)}), f32[1,2,8,32]{2,1,0,3:T(2,128)S(1)}, u32[]{:S(2)}, u32[]{:S(2)}) async-start(f32[1,2,8,32]{2,1,0,3:T(2,128)} %copy.56), calls=%async_computation.4 | async-start | bytes 65536 | tf_op jit(solution)/shard_map/all_to_all | solution.py:105
  31.0 0.2 fusion.37
  31.2 0.9 copy.43
  32.0 0.8 copy.54
  32.9 0.7 copy.61
  33.6 0.6 dynamic-slice.3
  34.8 0.8 copy.51
  35.6 0.1 all-to-all-done.4
  35.7 4.0 %all-to-all-start.5 = ((f32[1,2,8,32]{2,1,0,3:T(2,128)}), f32[1,2,8,32]{2,1,0,3:T(2,128)S(1)}, u32[]{:S(2)}, u32[]{:S(2)}) async-start(f32[1,2,8,32]{2,1,0,3:T(2,128)} %copy.61), calls=%async_computation.5 | async-start | bytes 65536 | tf_op jit(solution)/shard_map/all_to_all | solution.py:106
  39.8 4.8 %all-to-all-done.5 = f32[1,2,8,32]{2,1,0,3:T(2,128)S(1)} async-done(((f32[1,2,8,32]{2,1,0,3:T(2,128)}), f32[1,2,8,32]{2,1,0,3:T(2,128)S(1)}, u32[]{:S(2)}, u32[]{:S(2)}) %all-to-all-start.5) | async-done | bytes 2080 | tf_op jit(solution)/shard_map/all_to_all | solution.py:106
  44.6 3.4 %all-to-all-start = ((f32[1,2,8,32,128]{4,2,1,0,3:T(8,128)}), f32[1,2,8,32,128]{4,2,1,0,3:T(8,128)S(1)}, u32[]{:S(2)}, u32[]{:S(2)}) async-start(f32[1,2,8,32,128]{4,2,1,0,3:T(8,128)} %copy.43), calls=%async_computation | async-start | bytes 524288 | tf_op jit(solution)/shard_map/all_to_all | solution.py:104
  48.1 0.2 copy.47
  48.2 0.2 copy.58
  48.4 6.4 %all-to-all-done = f32[1,2,8,32,128]{4,2,1,0,3:T(8,128)S(1)} async-done(((f32[1,2,8,32,128]{4,2,1,0,3:T(8,128)}), f32[1,2,8,32,128]{4,2,1,0,3:T(8,128)S(1)}, u32[]{:S(2)}, u32[]{:S(2)}) %all-to-all-start) | async-done | bytes 262176 | tf_op jit(solution)/shard_map/all_to_all | solution.py:104
  54.8 3.4 %all-to-all-start.3 = ((f32[1,2,8,32,128]{4,2,1,0,3:T(8,128)}), f32[1,2,8,32,128]{4,2,1,0,3:T(8,128)S(1)}, u32[]{:S(2)}, u32[]{:S(2)}) async-start(f32[1,2,8,32,128]{4,2,1,0,3:T(8,128)} %copy.54), calls=%async_computation.3 | async-start | bytes 524288 | tf_op jit(solution)/shard_map/all_to_all | solution.py:107
  58.2 0.2 fusion.32
  58.5 0.2 fusion.15
  58.7 9.8 %all_gather.12 = bf16[2,32,1024]{2,0,1:T(2,128)(2,1)S(1)} all-gather(bf16[2,4,1024]{2,0,1:T(2,128)(2,1)S(1)} %copy.52), channel_id=1, replica_groups=mesh['seq'=8,'head'=4] {'seq'}, dimensions={1}, use_global_device_ids=true | all-gather | bytes 147456 | tf_op jit(solution)/shard_map/all_gather | solution.py:128
  68.6 16.5 %all_gather.13 = bf16[8,32,1024]{2,1,0:T(8,128)(2,1)S(1)} all-gather(bf16[2,32,1024]{2,1,0:T(8,128)(2,1)S(1)} %copy.53), channel_id=1, replica_groups=mesh['seq'=8,'head'=4] {'head'}, dimensions={0}, use_global_device_ids=true | all-gather | bytes 655360 | tf_op jit(solution)/shard_map/all_gather | solution.py:132
  85.0 0.0 all-to-all-done.3
  85.0 0.2 fusion.31
  85.3 0.2 fusion.16
  85.5 9.2 %all_gather.14 = bf16[2,32,1024]{2,0,1:T(2,128)(2,1)S(1)} all-gather(bf16[2,4,1024]{2,0,1:T(2,128)(2,1)S(1)} %copy.63), channel_id=1, replica_groups=mesh['seq'=8,'head'=4] {'seq'}, dimensions={1}, use_global_device_ids=true | all-gather | bytes 147456 | tf_op jit(solution)/shard_map/all_gather | solution.py:129
  94.7 16.5 %all_gather.15 = bf16[8,32,1024]{2,1,0:T(8,128)(2,1)S(1)} all-gather(bf16[2,32,1024]{2,1,0:T(8,128)(2,1)S(1)} %copy.64), channel_id=1, replica_groups=mesh['seq'=8,'head'=4] {'head'}, dimensions={0}, use_global_device_ids=true | all-gather | bytes 655360 | tf_op jit(solution)/shard_map/all_gather | solution.py:133
  111.2 0.1 maximum_bitcast_fusion
  111.3 0.6 copy.65
  111.9 0.5 reshape.148
  112.4 3.0 %fusion = f32[32,2,2048]{2,0,1:T(8,128)S(1)} fusion(bf16[1024,2048]{1,0:T(8,128)(2,1)} %param.15, bf16[32,2,8192]{2,0,1:T(8,128)(2,1)S(1)} %reshape.148, s32[]{:T(128)S(6)} %select_n.47), kind=kOutput, calls=%fused_computation | convolution fusion | flops 268435456 | bytes 4849668 | tf_op jit(solution)/shard_map/nrk,kd->nrd/dot_general | solution.py:143
  115.5 29.5 %all-reduce.2 = bf16[32,2,2048]{2,0,1:T(8,128)(2,1)S(1)} all-reduce(f32[32,2,2048]{2,0,1:T(8,128)S(1)} %fusion), channel_id=2, replica_groups=mesh['seq'=8,'head'=4] {'seq'}, use_global_device_ids=true, to_apply=%region_15.16.clone | all-reduce | flops 131072 | bytes 786432
  145.0 0.6 slice_bitcast_fusion
  (28 shorter events, 0.3 us)
Async XLA Ops:
  0.6 1.1 copy-start
  1.7 1.5 %copy-start.5 = (pred[1,2,8,128]{3,1,2,0:T(4,128)(4,1)}, pred[1,2,8,128]{3,1,2,0:T(4,128)(4,1)S(1)}, u32[]{:S(2)}) copy-start(pred[1,2,8,128]{3,1,2,0:T(4,128)(4,1)S(1)} %copy.92) | copy-start | bytes 6148
  1.7 9.4 %copy-start.2 = (bf16[2,2,8,32,128]{4,3,2,1,0:T(8,128)(2,1)S(1)}, bf16[2,2,8,32,128]{4,3,2,1,0:T(8,128)(2,1)}, u32[]{:S(2)}) copy-start(bf16[2,2,8,32,128]{4,3,2,1,0:T(8,128)(2,1)} %param.8) | copy-start | bytes 786436
  3.2 1.4 copy-start.1
  5.2 7.1 %copy-start.3 = (bf16[2,1024,128]{2,1,0:T(8,128)(2,1)S(1)}, bf16[2,1024,128]{2,1,0:T(8,128)(2,1)}, u32[]{:S(2)}) copy-start(bf16[2,1024,128]{2,1,0:T(8,128)(2,1)} %param.12) | copy-start | bytes 1572868
  5.9 12.7 %all-to-all-start.2 = ((f32[1,2,8,32]{2,1,0,3:T(2,128)}), f32[1,2,8,32]{2,1,0,3:T(2,128)}, u32[]{:S(2)}, u32[]{:S(2)}) async-start(f32[1,2,8,32]{2,1,0,3:T(2,128)} %copy.50), calls=%async_computation.2 | async-start | bytes 65536 | tf_op jit(solution)/shard_map/all_to_all | solution.py:103
  15.3 2.2 %copy-start.6 = (bf16[2,2,32,128]{3,2,1,0:T(8,128)(2,1)S(1)}, bf16[2,2,32,128]{3,2,1,0:T(8,128)(2,1)}, u32[]{:S(2)}) copy-start(bf16[2,2,32,128]{3,2,1,0:T(8,128)(2,1)} %param.9) | copy-start | bytes 98308
  16.1 1.8 %copy-start.7 = (pred[2,4,32]{2,1,0:T(4,128)(4,1)}, pred[2,4,32]{2,1,0:T(4,128)(4,1)S(1)}, u32[]{:S(2)}) copy-start(pred[2,4,32]{2,1,0:T(4,128)(4,1)S(1)} %fusion.67) | copy-start | bytes 772
  17.4 13.8 %copy-start.4 = (f32[1,2,8,32,128]{4,3,2,1,0:T(8,128)S(1)}, f32[1,2,8,32,128]{4,3,2,1,0:T(8,128)}, u32[]{:S(2)}) copy-start(f32[1,2,8,32,128]{4,3,2,1,0:T(8,128)} %convolution_bitcast_fusion.1) | copy-start | bytes 786436
  17.4 16.1 %copy-start.10 = (u32[32]{0:T(128)S(1)}, u32[32]{0:T(128)}, u32[]{:S(2)}) copy-start(u32[32]{0:T(128)} %constant.61) | copy-start | bytes 388
  17.9 13.1 %copy-start.8 = (pred[2,4,32]{2,1,0:T(4,128)(4,1)S(1)}, pred[2,4,32]{2,1,0:T(4,128)(4,1)}, u32[]{:S(2)}) copy-start(pred[2,4,32]{2,1,0:T(4,128)(4,1)} %copy-done.7) | copy-start | bytes 772
  18.6 9.0 %all-to-all-start.1 = ((f32[1,2,8,32]{2,1,0,3:T(2,128)}), f32[1,2,8,32]{2,1,0,3:T(2,128)S(1)}, u32[]{:S(2)}, u32[]{:S(2)}) async-start(f32[1,2,8,32]{2,1,0,3:T(2,128)} %copy.45), calls=%async_computation.1 | async-start | bytes 65536 | tf_op jit(solution)/shard_map/all_to_all | solution.py:102
  23.3 35.2 %copy-start.9 = (bf16[2,2,32,128]{3,2,1,0:T(8,128)(2,1)S(1)}, bf16[2,2,32,128]{3,2,1,0:T(8,128)(2,1)}, u32[]{:S(2)}) copy-start(bf16[2,2,32,128]{3,2,1,0:T(8,128)(2,1)} %param.10) | copy-start | bytes 98308
  27.6 8.1 %all-to-all-start.4 = ((f32[1,2,8,32]{2,1,0,3:T(2,128)}), f32[1,2,8,32]{2,1,0,3:T(2,128)S(1)}, u32[]{:S(2)}, u32[]{:S(2)}) async-start(f32[1,2,8,32]{2,1,0,3:T(2,128)} %copy.56), calls=%async_computation.4 | async-start | bytes 65536 | tf_op jit(solution)/shard_map/all_to_all | solution.py:105
  35.7 8.8 %all-to-all-start.5 = ((f32[1,2,8,32]{2,1,0,3:T(2,128)}), f32[1,2,8,32]{2,1,0,3:T(2,128)S(1)}, u32[]{:S(2)}, u32[]{:S(2)}) async-start(f32[1,2,8,32]{2,1,0,3:T(2,128)} %copy.61), calls=%async_computation.5 | async-start | bytes 65536 | tf_op jit(solution)/shard_map/all_to_all | solution.py:106
  44.6 10.3 %all-to-all-start = ((f32[1,2,8,32,128]{4,2,1,0,3:T(8,128)}), f32[1,2,8,32,128]{4,2,1,0,3:T(8,128)S(1)}, u32[]{:S(2)}, u32[]{:S(2)}) async-start(f32[1,2,8,32,128]{4,2,1,0,3:T(8,128)} %copy.43), calls=%async_computation | async-start | bytes 524288 | tf_op jit(solution)/shard_map/all_to_all | solution.py:104
  54.8 30.2 %all-to-all-start.3 = ((f32[1,2,8,32,128]{4,2,1,0,3:T(8,128)}), f32[1,2,8,32,128]{4,2,1,0,3:T(8,128)S(1)}, u32[]{:S(2)}, u32[]{:S(2)}) async-start(f32[1,2,8,32,128]{4,2,1,0,3:T(8,128)} %copy.54), calls=%async_computation.3 | async-start | bytes 524288 | tf_op jit(solution)/shard_map/all_to_all | solution.py:107
where the time goes:
time: 147 us; the launch traced here: 146 us
  blocking collectives  81.4 us (55%)
  starting transfers between devices  23.5 us (16%)
  waiting for transfers between devices  15 us (10%)
  local copies, waits for them, and re-layouts  11.7 us (8%)
  matrix products  9.38 us (6%)
  other arithmetic  2.98 us (2%)
  between operations  1.64 us (1%)
    unnamed x1, blocking collectives  29.5 us
    all_gather x1, blocking collectives, local(): lax.all_gather(verify_all, 'head', axis=0, tiled=True)  16.5 us
    all_gather x1, blocking collectives, local(): lax.all_gather(draft_all, 'head', axis=0, tiled=True)  16.5 us
    all_gather x1, blocking collectives, local(): lax.all_gather(finish(draft_cache, draft_tree), 'seq', axis=1, tiled=True)  9.83 us
    all_gather x1, blocking collectives, local(): lax.all_gather(finish(verify_cache, verify_tree), 'seq', axis=1, tiled=True)  9.17 us
    all_to_all x1, waiting for transfers between devices, local(): lax.all_to_all(draft_part[2][None], 'seq', split_axis=3, concat_axis=0, t...  6.41 us
    all_to_all x1, starting transfers between devices, local(): lax.all_to_all(draft_part[1][None], 'seq', split_axis=3, concat_axis=0, t...  5.2 us
    all_to_all x1, waiting for transfers between devices, local(): lax.all_to_all(verify_part[1][None], 'seq', split_axis=3, concat_axis=0,...  4.78 us
  transfers between devices with their start and end apart: 6, of which 4 were waited for; matrix products, arithmetic and copies ran while one was open for 9% of the time, Pallas kernels for 0%

commit v1 on v0

v1 whole, which is shorter than its diff:
```python
import functools
import math

import jax
import jax.numpy as jnp
import numpy as np
from jax import lax
from jax.experimental import pallas as pl
from jax.experimental.pallas import tpu as pltpu
from jax.sharding import PartitionSpec as P

KVH = 8
BLOCK = 128
MESH = pl.DeviceIdType.MESH
F32 = jnp.float32
BF16 = jnp.bfloat16


def flip(index, mask):
    out = index
    bit = 1
    while bit <= mask:
        if mask & bit:
            out = out + bit * (1 - 2 * ((index // bit) % 2))
        bit *= 2
    return out


def contract(left, right, left_dim, right_dim):
    return lax.dot_general(
        left, right, (((left_dim,), (right_dim,)), ((), ())), preferred_element_type=F32
    )


def kernel(
    dims,
    ids_ref,
    anc_ref,
    spread_ref,
    order_ref,
    tk_ref,
    tv_ref,
    q_hbm,
    k_hbm,
    v_hbm,
    w_hbm,
    draft_ref,
    verify_ref,
    q_v,
    k_v,
    v_v,
    w_v,
    acc_out,
    stat_out,
    acc_in,
    stat_in,
    zbuf,
    parts,
    mix_out,
    mix_in,
    load_sem,
    s1,
    r1,
    s1s,
    r1s,
    s2,
    r2,
    s3,
    r3,
    s4,
    r4,
):
    seq_n, head_n, pair_dev, groups, nodes, requests, hd, heads_dev = dims
    me = lax.axis_index("seq")
    z = lax.axis_index("head")
    blocks = 2 * pair_dev
    per_block = seq_n // blocks
    rows = groups * nodes
    chunk = rows // per_block
    chunk_heads = chunk // nodes
    pieces = heads_dev // chunk_heads
    ctx = k_v.shape[1]
    blocks_dev = ctx // BLOCK
    node_dev = nodes // seq_n
    out_rows = 2 * node_dev * requests
    factor2 = hd ** (-0.5) * math.log2(math.e)

    loads = []
    for i, (src, dst) in enumerate(((k_hbm, k_v), (q_hbm, q_v), (v_hbm, v_v), (w_hbm, w_v))):
        copy = pltpu.make_async_copy(src, dst, load_sem.at[i])
        copy.start()
        loads.append(copy)

    barrier = pltpu.get_barrier_semaphore()
    for k in range(1, seq_n):
        pl.semaphore_signal(barrier, inc=1, device_id={"seq": flip(me, k)}, device_id_type=MESH)
    for k in range(1, head_n):
        pl.semaphore_signal(barrier, inc=1, device_id={"head": flip(z, k)}, device_id_type=MESH)

    loads[0].wait()
    loads[1].wait()
    own_block = me // per_block
    own_piece = me % per_block
    owned = me * blocks_dev + lax.broadcasted_iota(jnp.int32, (blocks_dev, 1), 0)

    sends = []
    for step in reversed(range(blocks)):
        block = flip(own_block, step)
        attention = block // pair_dev
        pair = block % pair_dev
        hit = (ids_ref[pair] == owned).astype(F32)
        chosen = jnp.max(hit, axis=1, keepdims=True)
        chosen = jnp.maximum(chosen, attention.astype(F32))
        bias = (chosen - 1.0) * 1e30
        scores = contract(k_v[pair], q_v[block], 1, 1)
        masked = [
            scores[b * BLOCK : (b + 1) * BLOCK] + bias[b : b + 1, :] for b in range(blocks_dev)
        ]
        top = functools.reduce(jnp.maximum, masked)
        peak = jnp.max(top, axis=0, keepdims=True)
        weights = [jnp.exp2((part - peak) * factor2) for part in masked]
        total = jnp.sum(functools.reduce(jnp.add, weights), axis=0, keepdims=True)
        rounded = jnp.concatenate([part.astype(BF16) for part in weights], axis=0)
        if step == blocks - 1:
            loads[2].wait()
        summed = contract(v_v[pair], rounded, 0, 0)
        for piece in range(per_block):
            columns = slice(piece * chunk, (piece + 1) * chunk)
            acc_out[step, piece] = summed[:, columns].astype(BF16)
            stat_out[step, piece, 0:1, :] = peak[:, columns]
            stat_out[step, piece, 1:2, :] = total[:, columns]
        if step == blocks - 1:
            pl.semaphore_wait(barrier, seq_n + head_n - 2)
        for j in range(per_block):
            k = step * per_block + j
            if k == 0:
                continue
            piece = flip(own_piece, j)
            target = flip(me, k)
            for src, dst, ss, rs in (
                (acc_out, acc_in, s1, r1),
                (stat_out, stat_in, s1s, r1s),
            ):
                copy = pltpu.make_async_remote_copy(
                    src_ref=src.at[step, piece],
                    dst_ref=dst.at[k],
                    send_sem=ss.at[k],
                    recv_sem=rs.at[k],
                    device_id={"seq": target},
                    device_id_type=MESH,
                )
                copy.start()
                sends.append(copy)
    first = list(sends)

    own_attention = own_block // pair_dev
    own_pair = own_block % pair_dev
    request = (z * pair_dev + own_pair) // KVH
    own_rows = q_v[own_block, pl.ds(pl.multiple_of(own_piece * chunk, chunk), chunk), :]
    tree_scores = contract(tk_ref[own_block], own_rows, 1, 1)
    allowed = contract(anc_ref[request].astype(F32).astype(BF16), spread_ref[...], 0, 0)
    tree_scores = jnp.where(allowed > 0.5, tree_scores, -1e30)
    tree_peak = jnp.max(tree_scores, axis=0, keepdims=True)
    tree_weights = jnp.exp2((tree_scores - tree_peak) * factor2)
    tree_total = jnp.sum(tree_weights, axis=0, keepdims=True)
    tree_sum = contract(tv_ref[own_block], tree_weights.astype(BF16), 0, 0)

    for copy in first:
        copy.wait_recv()
    peaks = [tree_peak, stat_out[0, own_piece, 0:1, :]]
    totals = [tree_total, stat_out[0, own_piece, 1:2, :]]
    for k in range(1, seq_n):
        peaks.append(stat_in[k, 0:1, :])
        totals.append(stat_in[k, 1:2, :])
    highest = functools.reduce(jnp.maximum, peaks)
    factors = [jnp.exp2((peak - highest) * factor2) for peak in peaks]
    total = functools.reduce(jnp.add, [t * f for t, f in zip(totals, factors)])
    summed = tree_sum * factors[0] + acc_out[0, own_piece].astype(F32) * factors[1]
    for k in range(1, seq_n):
        summed = summed + acc_in[k].astype(F32) * factors[k + 1]
    zbuf[0] = jnp.transpose(summed / total).astype(BF16)

    hops = []
    for k in range(1, head_n):
        copy = pltpu.make_async_remote_copy(
            src_ref=zbuf.at[0],
            dst_ref=zbuf.at[k],
            send_sem=s2.at[k],
            recv_sem=r2.at[k],
            device_id={"head": flip(z, k)},
            device_id_type=MESH,
        )
        copy.start()
        hops.append(copy)
    routes = []
    for k in range(head_n):
        if k > 0:
            hops[k - 1].wait_recv()
        origin = flip(z, k)
        whole_pair = origin * pair_dev + own_pair
        first_head = (whole_pair % KVH) * groups + own_piece * chunk_heads
        target = first_head // heads_dev
        slot = (own_attention * requests + whole_pair // KVH) * pieces + (
            first_head % heads_dev
        ) // chunk_heads

        remote = pltpu.make_async_remote_copy(
            src_ref=zbuf.at[k],
            dst_ref=parts.at[slot],
            send_sem=s3.at[k],
            recv_sem=r3.at[slot],
            device_id={"seq": target},
            device_id_type=MESH,
        )
        here = pltpu.make_async_copy(zbuf.at[k], parts.at[slot], r3.at[slot])

        @pl.when(target != me)
        def _():
            remote.start()

        @pl.when(target == me)
        def _():
            here.start()

        routes.append((target, remote))

    loads[3].wait()
    for slot in range(2 * requests * pieces):
        pltpu.make_async_copy(zbuf.at[0], parts.at[slot], r3.at[slot]).wait()
    stacked = jnp.concatenate(
        [
            jnp.concatenate(
                [
                    parts[lead * pieces + piece, h * nodes : (h + 1) * nodes, :]
                    for piece in range(pieces)
                    for h in range(chunk_heads)
                ],
                axis=1,
            )
            for lead in range(2 * requests)
        ],
        axis=0,
    )
    ordered = contract(order_ref[...], stacked, 1, 0).astype(BF16)
    columns = w_v.shape[1]
    halves = mix_out.shape[0]
    width = columns // halves
    last = []
    for half in range(halves):
        mixed = contract(ordered, w_v[:, half * width : (half + 1) * width], 1, 0)
        for t in range(seq_n):
            mix_out[half, t] = mixed[t * out_rows : (t + 1) * out_rows].astype(BF16)
        for k in reversed(range(1, seq_n)):
            target = flip(me, k)
            copy = pltpu.make_async_remote_copy(
                src_ref=mix_out.at[half, target],
                dst_ref=mix_in.at[half, k],
                send_sem=s4.at[half, k],
                recv_sem=r4.at[half, k],
                device_id={"seq": target},
                device_id_type=MESH,
            )
            copy.start()
            last.append((half, copy))
    for half in range(halves):
        for h, copy in last:
            if h == half:
                copy.wait_recv()
        result = mix_out[half, me].astype(F32)
        for k in range(1, seq_n):
            result = result + mix_in[half, k].astype(F32)
        span = slice(half * width, (half + 1) * width)
        draft_ref[:, span] = result[: out_rows // 2].astype(BF16)
        verify_ref[:, span] = result[out_rows // 2 :].astype(BF16)

    for copy in first:
        copy.wait_send()
    for copy in hops:
        copy.wait_send()
    for target, remote in routes:

        @pl.when(target != me)
        def _():
            remote.wait_send()

    for _, copy in last:
        copy.wait_send()


def local(
    queries, tree_keys, tree_values, cache_keys, cache_values, block_ids, ancestors, out_weight
):
    _, pair_dev, groups, nodes, hd = queries.shape
    ctx = cache_keys.shape[1]
    requests = ancestors.shape[0]
    rows_dev, columns = out_weight.shape
    seq_n = lax.axis_size("seq")
    head_n = lax.axis_size("head")
    heads_dev = rows_dev // hd
    blocks = 2 * pair_dev
    per_block = seq_n // blocks
    rows = groups * nodes
    chunk = rows // per_block
    node_dev = nodes // seq_n
    halves = 2
    width = columns // halves
    out_rows = 2 * node_dev * requests
    all_rows = 2 * requests * nodes
    slots = 2 * requests * heads_dev * nodes // chunk

    spread = (np.arange(chunk)[None, :] % nodes == np.arange(nodes)[:, None]).astype(np.float32)
    order = np.zeros((all_rows, all_rows), np.float32)
    for a in range(2):
        for r in range(requests):
            for n in range(nodes):
                t, j = divmod(n, node_dev)
                row = t * out_rows + a * (node_dev * requests) + j * requests + r
                order[row, (a * requests + r) * nodes + n] = 1.0

    dims = (seq_n, head_n, pair_dev, groups, nodes, requests, hd, heads_dev)
    vmem = pl.BlockSpec(memory_space=pltpu.VMEM)
    anywhere = pl.BlockSpec(memory_space=pl.ANY)
    shape = jax.ShapeDtypeStruct((node_dev * requests, columns), BF16)
    dma = pltpu.SemaphoreType.DMA
    draft, verify = pl.pallas_call(
        functools.partial(kernel, dims),
        out_shape=(shape, shape),
        in_specs=[vmem] * 6 + [anywhere] * 4,
        out_specs=(vmem, vmem),
        scratch_shapes=[
            pltpu.VMEM((blocks, rows, hd), BF16),
            pltpu.VMEM((pair_dev, ctx, hd), BF16),
            pltpu.VMEM((pair_dev, ctx, hd), BF16),
            pltpu.VMEM((rows_dev, columns), BF16),
            pltpu.VMEM((blocks, per_block, hd, chunk), BF16),
            pltpu.VMEM((blocks, per_block, 8, chunk), F32),
            pltpu.VMEM((seq_n, hd, chunk), BF16),
            pltpu.VMEM((seq_n, 8, chunk), F32),
            pltpu.VMEM((head_n, chunk, hd), BF16),
            pltpu.VMEM((slots, chunk, hd), BF16),
            pltpu.VMEM((halves, seq_n, out_rows, width), BF16),
            pltpu.VMEM((halves, seq_n, out_rows, width), BF16),
            dma((4,)),
            dma((seq_n,)),
            dma((seq_n,)),
            dma((seq_n,)),
            dma((seq_n,)),
            dma((head_n,)),
            dma((head_n,)),
            dma((head_n,)),
            dma((slots,)),
            dma((halves, seq_n)),
            dma((halves, seq_n)),
        ],
        compiler_params=pltpu.CompilerParams(
            collective_id=0, has_side_effects=True, vmem_limit_bytes=40 * 1024 * 1024
        ),
        name="tree_attention",
    )(
        block_ids.reshape(pair_dev, 1, block_ids.shape[1]),
        ancestors,
        jnp.asarray(spread, BF16),
        jnp.asarray(order, BF16),
        tree_keys.reshape(blocks, nodes, hd),
        tree_values.reshape(blocks, nodes, hd),
        queries.reshape(blocks, rows, hd),
        cache_keys,
        cache_values,
        out_weight,
    )
    final = (node_dev, requests, columns)
    return draft.reshape(final), verify.reshape(final)


def solution(mesh):
    in_specs = (
        P(None, "head", None, None, None),
        P(None, "head", None, None),
        P(None, "head", None, None),
        P("head", "seq", None),
        P("head", "seq", None),
        P("head", None),
        P(),
        P("seq", "head"),
    )
    out_specs = (P("seq", None, "head"), P("seq", None, "head"))
    return jax.shard_map(local, mesh=mesh, in_specs=in_specs, out_specs=out_specs, check_vma=False)
```

time: 147 us -> 38.1 us (0.26)
  blocking collectives: 81.4 us -> 0 us
  Pallas kernels: 0 us -> 26.1 us
  starting transfers between devices: 23.5 us -> 0 us
  waiting for transfers between devices: 15 us -> 0 us
  matrix products: 9.38 us -> 0 us
  other arithmetic: 2.98 us -> 0 us
    all_gather x4 -> x0, blocking collectives: 52 us -> none  [the longest x1 16.5 us: local(): lax.all_gather(verify_all, 'head', axis=0, tiled=True)]
    unnamed x1 -> x0, blocking collectives: 29.5 us -> none
    pallas_call x0 -> x1, Pallas kernels: none -> 26.1 us  [local(): pl.pallas_call(functools.partial(kernel, dims), out_shape=(shape, shape),...]
    all_to_all x6 -> x0, starting transfers between devices: 23.5 us -> none  [the longest x1 5.2 us: local(): lax.all_to_all(draft_part[1][None], 'seq', split_axis=3, concat_axis=0, t...]
    all_to_all x6 -> x0, waiting for transfers between devices: 15 us -> none  [the longest x1 6.41 us: local(): lax.all_to_all(draft_part[2][None], 'seq', split_axis=3, concat_axis=0, t...]
    dot_general x9 -> x0, matrix products: 9.38 us -> none  [the longest x2 3.54 us: cache_partial(): jnp.einsum('pgnl,plh->pgnh', weights.astype(jnp.bfloat16), value_rows, pr...]
    unnamed x25 -> x22, local copies, waits for them, and re-layouts: 2.07 us -> 10.7 us
    broadcast_in_dim x6 -> x0, local copies, waits for them, and re-layouts: 4.46 us -> none  [the longest x1 0.86 us: local(): draft_part[2][None]]
  transfers between devices with their start and end apart: 6 -> 0, of which waited for: 4 -> 0; matrix products, arithmetic and copies ran while one was open for 9% -> 0% of each run, Pallas kernels for 0% -> 0%
where the time goes in v1:
time: 38.1 us; the launch traced here: 37.5 us
  Pallas kernels  26.1 us (69%)
  local copies, waits for them, and re-layouts  10.7 us (28%)
  between operations  0.66 us (2%)
    pallas_call x1, Pallas kernels, local(): pl.pallas_call(functools.partial(kernel, dims), out_shape=(shape, shape),...  26.1 us
    unnamed x22, local copies, waits for them, and re-layouts  10.7 us

profile of v1, /device:TPU:0, one launch (start us, length us, event | category | flops | bytes accessed | tf_op | source)
XLA Modules:
  0.0 37.5 jit_solution(3263233447471714646)
XLA Ops:
  0.6 0.0 copy-start
  0.6 2.2 %copy-done = bf16[1024,2048]{1,0:T(8,128)(2,1)S(1)} copy-done((bf16[1024,2048]{1,0:T(8,128)(2,1)S(1)}, bf16[1024,2048]{1,0:T(8,128)(2,1)}, u32[]{:S(2)}) %copy-start) | copy-done | bytes 4194328
  2.8 0.0 copy-start.1
  2.8 1.0 %copy-done.1 = bf16[2,1024,128]{2,1,0:T(8,128)(2,1)S(1)} copy-done((bf16[2,1024,128]{2,1,0:T(8,128)(2,1)S(1)}, bf16[2,1024,128]{2,1,0:T(8,128)(2,1)}, u32[]{:S(2)}) %copy-start.1) | copy-done | bytes 524312
  3.9 0.0 copy-start.2
  3.9 1.0 %copy-done.2 = bf16[2,1024,128]{2,1,0:T(8,128)(2,1)S(1)} copy-done((bf16[2,1024,128]{2,1,0:T(8,128)(2,1)S(1)}, bf16[2,1024,128]{2,1,0:T(8,128)(2,1)}, u32[]{:S(2)}) %copy-start.2) | copy-done | bytes 524312
  4.9 0.0 copy-start.3
  4.9 0.9 %copy-done.3 = bf16[2,2,8,32,128]{4,3,2,1,0:T(8,128)(2,1)S(1)} copy-done((bf16[2,2,8,32,128]{4,3,2,1,0:T(8,128)(2,1)S(1)}, bf16[2,2,8,32,128]{4,3,2,1,0:T(8,128)(2,1)}, u32[]{:S(2)}) %copy-start.3) | copy-done | bytes 262168
  5.9 0.0 copy-start.4
  5.9 0.8 %copy-done.4 = bf16[2,2,32,128]{3,2,1,0:T(8,128)(2,1)S(1)} copy-done((bf16[2,2,32,128]{3,2,1,0:T(8,128)(2,1)S(1)}, bf16[2,2,32,128]{3,2,1,0:T(8,128)(2,1)}, u32[]{:S(2)}) %copy-start.4) | copy-done | bytes 32792
  6.6 0.0 copy-start.5
  6.6 0.8 %copy-done.5 = bf16[2,2,32,128]{3,2,1,0:T(8,128)(2,1)S(1)} copy-done((bf16[2,2,32,128]{3,2,1,0:T(8,128)(2,1)S(1)}, bf16[2,2,32,128]{3,2,1,0:T(8,128)(2,1)}, u32[]{:S(2)}) %copy-start.5) | copy-done | bytes 32792
  7.4 0.0 copy-start.6
  7.4 0.7 %copy-done.6 = s32[1,32,32]{2,1,0:T(8,128)S(1)} copy-done((s32[1,32,32]{2,1,0:T(8,128)S(1)}, s32[1,32,32]{2,1,0:T(8,128)}, u32[]{:S(2)}) %copy-start.6) | copy-done | bytes 4120
  8.1 0.0 copy-start.7
  8.1 0.7 %copy-done.7 = bf16[64,64]{1,0:T(8,128)(2,1)S(1)} copy-done((bf16[64,64]{1,0:T(8,128)(2,1)S(1)}, bf16[64,64]{1,0:T(8,128)(2,1)}, u32[]{:S(2)}) %copy-start.7) | copy-done | bytes 8216
  8.8 0.0 copy-start.8
  8.8 0.7 %copy-done.8 = bf16[32,128]{1,0:T(8,128)(2,1)S(1)} copy-done((bf16[32,128]{1,0:T(8,128)(2,1)S(1)}, bf16[32,128]{1,0:T(8,128)(2,1)}, u32[]{:S(2)}) %copy-start.8) | copy-done | bytes 8216
  9.5 0.0 copy-start.9
  9.5 0.7 %copy-done.9 = s32[2,32]{1,0:T(2,128)S(1)} copy-done((s32[2,32]{1,0:T(2,128)S(1)}, s32[2,32]{1,0:T(2,128)}, u32[]{:S(2)}) %copy-start.9) | copy-done | bytes 280
  10.2 26.1 %tree_attention.1 = (bf16[4,2048]{1,0:T(4,128)(2,1)S(1)}, bf16[4,2048]{1,0:T(4,128)(2,1)S(1)}) custom-call(s32[2,1,32]{2,1,0:T(1,128)S(1)} %bitcast.13, s32[1,32,32]{2,1,0:T(8,128)S(1)} %copy-done.6, bf16[32,128]{1,0:T(8,128)(2,1)S(1)} %copy-done.8, bf16[64,64]{1,0:T(8,128)(2,1)S(1)} %copy-done.7, bf16[4,32,128]{2,1,0:T(8,128)(2,1)S(1)} %bitcast.9, ...), custom_call_target="tpu_custom_call" | custom-call | tf_op jit(solution)/shard_map/tree_attention/pallas_call | solution.py:325
  36.3 0.6 %copy.15 = bf16[4,1,2048]{2,0,1:T(4,128)(2,1)} copy(bf16[4,1,2048]{2,0,1:T(4,128)(2,1)S(1)} %bitcast.12) | data formatting | bytes 32768
  36.9 0.6 %copy.16 = bf16[4,1,2048]{2,0,1:T(4,128)(2,1)} copy(bf16[4,1,2048]{2,0,1:T(4,128)(2,1)S(1)} %bitcast.11) | data formatting | bytes 32768
Async XLA Ops:
  0.6 2.2 %copy-start = (bf16[1024,2048]{1,0:T(8,128)(2,1)S(1)}, bf16[1024,2048]{1,0:T(8,128)(2,1)}, u32[]{:S(2)}) copy-start(bf16[1024,2048]{1,0:T(8,128)(2,1)} %w_hbm.1) | copy-start | bytes 12582916
  2.8 1.0 %copy-start.1 = (bf16[2,1024,128]{2,1,0:T(8,128)(2,1)S(1)}, bf16[2,1024,128]{2,1,0:T(8,128)(2,1)}, u32[]{:S(2)}) copy-start(bf16[2,1024,128]{2,1,0:T(8,128)(2,1)} %k_hbm.1) | copy-start | bytes 1572868
  3.9 1.0 %copy-start.2 = (bf16[2,1024,128]{2,1,0:T(8,128)(2,1)S(1)}, bf16[2,1024,128]{2,1,0:T(8,128)(2,1)}, u32[]{:S(2)}) copy-start(bf16[2,1024,128]{2,1,0:T(8,128)(2,1)} %v_hbm.1) | copy-start | bytes 1572868
  4.9 0.9 %copy-start.3 = (bf16[2,2,8,32,128]{4,3,2,1,0:T(8,128)(2,1)S(1)}, bf16[2,2,8,32,128]{4,3,2,1,0:T(8,128)(2,1)}, u32[]{:S(2)}) copy-start(bf16[2,2,8,32,128]{4,3,2,1,0:T(8,128)(2,1)} %param.10) | copy-start | bytes 786436
  5.9 0.8 %copy-start.4 = (bf16[2,2,32,128]{3,2,1,0:T(8,128)(2,1)S(1)}, bf16[2,2,32,128]{3,2,1,0:T(8,128)(2,1)}, u32[]{:S(2)}) copy-start(bf16[2,2,32,128]{3,2,1,0:T(8,128)(2,1)} %param.11) | copy-start | bytes 98308
  6.6 0.8 %copy-start.5 = (bf16[2,2,32,128]{3,2,1,0:T(8,128)(2,1)S(1)}, bf16[2,2,32,128]{3,2,1,0:T(8,128)(2,1)}, u32[]{:S(2)}) copy-start(bf16[2,2,32,128]{3,2,1,0:T(8,128)(2,1)} %param.12) | copy-start | bytes 98308
  7.4 0.7 %copy-start.6 = (s32[1,32,32]{2,1,0:T(8,128)S(1)}, s32[1,32,32]{2,1,0:T(8,128)}, u32[]{:S(2)}) copy-start(s32[1,32,32]{2,1,0:T(8,128)} %anc_ref.1) | copy-start | bytes 12292
  8.1 0.7 %copy-start.7 = (bf16[64,64]{1,0:T(8,128)(2,1)S(1)}, bf16[64,64]{1,0:T(8,128)(2,1)}, u32[]{:S(2)}) copy-start(bf16[64,64]{1,0:T(8,128)(2,1)} %constant.5.clone.order_ref) | copy-start | bytes 24580
  8.8 0.7 %copy-start.8 = (bf16[32,128]{1,0:T(8,128)(2,1)S(1)}, bf16[32,128]{1,0:T(8,128)(2,1)}, u32[]{:S(2)}) copy-start(bf16[32,128]{1,0:T(8,128)(2,1)} %constant.4.clone.spread_ref) | copy-start | bytes 24580
  9.5 0.7 %copy-start.9 = (s32[2,32]{1,0:T(2,128)S(1)}, s32[2,32]{1,0:T(2,128)}, u32[]{:S(2)}) copy-start(s32[2,32]{1,0:T(2,128)} %param.15) | copy-start | bytes 772

commit v2 on v1

--- a/solution.py
+++ b/solution.py
@@ -34,18 +34,23 @@
 
 def kernel(
     dims,
+    ids_hbm,
+    anc_hbm,
+    spread_hbm,
+    order_hbm,
+    tk_hbm,
+    tv_hbm,
+    q_hbm,
+    k_hbm,
+    v_hbm,
+    w_hbm,
+    out_ref,
     ids_ref,
     anc_ref,
     spread_ref,
     order_ref,
     tk_ref,
     tv_ref,
-    q_hbm,
-    k_hbm,
-    v_hbm,
-    w_hbm,
-    draft_ref,
-    verify_ref,
     q_v,
     k_v,
     v_v,
@@ -86,7 +91,9 @@
     factor2 = hd ** (-0.5) * math.log2(math.e)
 
     loads = []
-    for i, (src, dst) in enumerate(((k_hbm, k_v), (q_hbm, q_v), (v_hbm, v_v), (w_hbm, w_v))):
+    sources = (ids_hbm, q_hbm, k_hbm, v_hbm, tk_hbm, tv_hbm, anc_hbm, spread_hbm, order_hbm, w_hbm)
+    places = (ids_ref, q_v, k_v, v_v, tk_ref, tv_ref, anc_ref, spread_ref, order_ref, w_v)
+    for i, (src, dst) in enumerate(zip(sources, places)):
         copy = pltpu.make_async_copy(src, dst, load_sem.at[i])
         copy.start()
         loads.append(copy)
@@ -97,8 +104,8 @@
     for k in range(1, head_n):
         pl.semaphore_signal(barrier, inc=1, device_id={"head": flip(z, k)}, device_id_type=MESH)
 
-    loads[0].wait()
-    loads[1].wait()
+    for copy in loads[:3]:
+        copy.wait()
     own_block = me // per_block
     own_piece = me % per_block
     owned = me * blocks_dev + lax.broadcasted_iota(jnp.int32, (blocks_dev, 1), 0)
@@ -122,7 +129,7 @@
         total = jnp.sum(functools.reduce(jnp.add, weights), axis=0, keepdims=True)
         rounded = jnp.concatenate([part.astype(BF16) for part in weights], axis=0)
         if step == blocks - 1:
-            loads[2].wait()
+            loads[3].wait()
         summed = contract(v_v[pair], rounded, 0, 0)
         for piece in range(per_block):
             columns = slice(piece * chunk, (piece + 1) * chunk)
@@ -153,6 +160,8 @@
                 sends.append(copy)
     first = list(sends)
 
+    for copy in loads[4:8]:
+        copy.wait()
     own_attention = own_block // pair_dev
     own_pair = own_block % pair_dev
     request = (z * pair_dev + own_pair) // KVH
@@ -224,7 +233,8 @@
 
         routes.append((target, remote))
 
-    loads[3].wait()
+    for copy in loads[8:]:
+        copy.wait()
     for slot in range(2 * requests * pieces):
         pltpu.make_async_copy(zbuf.at[0], parts.at[slot], r3.at[slot]).wait()
     stacked = jnp.concatenate(
@@ -270,8 +280,7 @@
         for k in range(1, seq_n):
             result = result + mix_in[half, k].astype(F32)
         span = slice(half * width, (half + 1) * width)
-        draft_ref[:, span] = result[: out_rows // 2].astype(BF16)
-        verify_ref[:, span] = result[out_rows // 2 :].astype(BF16)
+        out_ref[:, span] = result.astype(BF16)
 
     for copy in first:
         copy.wait_send()
@@ -319,15 +328,21 @@
 
     dims = (seq_n, head_n, pair_dev, groups, nodes, requests, hd, heads_dev)
     vmem = pl.BlockSpec(memory_space=pltpu.VMEM)
-    anywhere = pl.BlockSpec(memory_space=pl.ANY)
-    shape = jax.ShapeDtypeStruct((node_dev * requests, columns), BF16)
+    hbm = pl.BlockSpec(memory_space=pltpu.HBM)
+    shape = jax.ShapeDtypeStruct((out_rows, columns), BF16)
     dma = pltpu.SemaphoreType.DMA
-    draft, verify = pl.pallas_call(
+    mixed = pl.pallas_call(
         functools.partial(kernel, dims),
-        out_shape=(shape, shape),
-        in_specs=[vmem] * 6 + [anywhere] * 4,
-        out_specs=(vmem, vmem),
+        out_shape=shape,
+        in_specs=[hbm] * 10,
+        out_specs=vmem,
         scratch_shapes=[
+            pltpu.VMEM((pair_dev, 1, block_ids.shape[1]), jnp.int32),
+            pltpu.VMEM((requests, nodes, nodes), jnp.int32),
+            pltpu.VMEM(spread.shape, BF16),
+            pltpu.VMEM(order.shape, BF16),
+            pltpu.VMEM((blocks, nodes, hd), BF16),
+            pltpu.VMEM((blocks, nodes, hd), BF16),
             pltpu.VMEM((blocks, rows, hd), BF16),
             pltpu.VMEM((pair_dev, ctx, hd), BF16),
             pltpu.VMEM((pair_dev, ctx, hd), BF16),
@@ -340,7 +355,7 @@
             pltpu.VMEM((slots, chunk, hd), BF16),
             pltpu.VMEM((halves, seq_n, out_rows, width), BF16),
             pltpu.VMEM((halves, seq_n, out_rows, width), BF16),
-            dma((4,)),
+            dma((10,)),
             dma((seq_n,)),
             dma((seq_n,)),
             dma((seq_n,)),
@@ -353,7 +368,7 @@
             dma((halves, seq_n)),
         ],
         compiler_params=pltpu.CompilerParams(
-            collective_id=0, has_side_effects=True, vmem_limit_bytes=40 * 1024 * 1024
+            collective_id=0, has_side_effects=True, vmem_limit_bytes=64 * 1000 * 1000
         ),
         name="tree_attention",
     )(
@@ -369,7 +384,8 @@
         out_weight,
     )
     final = (node_dev, requests, columns)
-    return draft.reshape(final), verify.reshape(final)
+    mixed = mixed.reshape((2,) + final)
+    return mixed[0], mixed[1]
 
 
 def solution(mesh):

time: 38.1 us -> 29.7 us (0.78); the launches traced: 37.5 us -> 29.5 us
  local copies, waits for them, and re-layouts: 10.7 us -> 1.46 us
  Pallas kernels: 26.1 us -> 27.4 us
    unnamed x22 -> x0, local copies, waits for them, and re-layouts: 10.7 us -> none
    squeeze x0 -> x1, local copies, waits for them, and re-layouts: none -> 1.46 us  [local(): return (mixed[0], mixed[1])]
    pallas_call x1, Pallas kernels: 26.1 us -> 27.4 us  [local(): pl.pallas_call(functools.partial(kernel, dims), out_shape=shape, in_specs...]
where the time goes in v2:
time: 29.7 us; the launch traced here: 29.5 us
  Pallas kernels  27.4 us (92%)
  local copies, waits for them, and re-layouts  1.46 us (5%)
  between operations  0.64 us (2%)
    pallas_call x1, Pallas kernels, local(): pl.pallas_call(functools.partial(kernel, dims), out_shape=shape, in_specs...  27.4 us
    squeeze x1, local copies, waits for them, and re-layouts, local(): return (mixed[0], mixed[1])  1.46 us

profile of v2, /device:TPU:0, one launch (start us, length us, event | category | flops | bytes accessed | tf_op | source)
XLA Modules:
  0.0 29.5 jit_solution(13735197408618502214)
XLA Ops:
  0.6 27.4 %tree_attention.1 = bf16[8,2048]{1,0:T(8,128)(2,1)} custom-call(s32[2,1,32]{2,1,0:T(1,128)} %bitcast.13, s32[1,32,32]{2,1,0:T(8,128)} %anc_hbm.1, bf16[32,128]{1,0:T(8,128)(2,1)} %constant.4.clone.spread_hbm, bf16[64,64]{1,0:T(8,128)(2,1)} %constant.5.clone.order_hbm, bf16[4,32,128]{2,1,0:T(8,128)(2,1)} %bitcast.11, bf16[4,32,128]{2,1,0:T(8,128)(2,1)} %bitcast.12, ...), custom_call_target="tpu_custom_call" | custom-call | tf_op jit(solution)/shard_map/tree_attention/pallas_call | solution.py:334
  28.0 1.5 %slice_bitcast_fusion = (bf16[4,1,2048]{2,0,1:T(4,128)(2,1)}, bf16[4,1,2048]{2,0,1:T(4,128)(2,1)}) fusion(bf16[8,2048]{1,0:T(8,128)(2,1)} %tree_attention.1), kind=kLoop, calls=%fused_computation | loop fusion | bytes 65536 | tf_op jit(solution)/shard_map/squeeze | solution.py:388

commit v3 on v2

--- a/solution.py
+++ b/solution.py
@@ -59,7 +59,7 @@
     stat_out,
     acc_in,
     stat_in,
-    zbuf,
+    done_rows,
     parts,
     mix_out,
     mix_in,
@@ -70,8 +70,6 @@
     r1s,
     s2,
     r2,
-    s3,
-    r3,
     s4,
     r4,
 ):
@@ -95,19 +93,54 @@
     places = (ids_ref, q_v, k_v, v_v, tk_ref, tv_ref, anc_ref, spread_ref, order_ref, w_v)
     for i, (src, dst) in enumerate(zip(sources, places)):
         copy = pltpu.make_async_copy(src, dst, load_sem.at[i])
-        copy.start()
+        if i < len(places) - 1:
+            copy.start()
         loads.append(copy)
 
     barrier = pltpu.get_barrier_semaphore()
     for k in range(1, seq_n):
         pl.semaphore_signal(barrier, inc=1, device_id={"seq": flip(me, k)}, device_id_type=MESH)
+    own_block = me // per_block
+    own_piece = me % per_block
+    own_attention = own_block // pair_dev
+    own_pair = own_block % pair_dev
+    own_whole = z * pair_dev + own_pair
+    first_head = (own_whole % KVH) * groups + own_piece * chunk_heads
+    holder = first_head // heads_dev
+    slot = (own_attention * requests + own_whole // KVH) * pieces + (
+        first_head % heads_dev
+    ) // chunk_heads
     for k in range(1, head_n):
-        pl.semaphore_signal(barrier, inc=1, device_id={"head": flip(z, k)}, device_id_type=MESH)
+        pl.semaphore_signal(
+            barrier,
+            inc=1,
+            device_id={"seq": holder, "head": flip(z, k)},
+            device_id_type=MESH,
+        )
+    greeted = seq_n + head_n - 2
+    own_kv = (me * heads_dev) // groups
+    base_piece = (me * heads_dev) % groups // chunk_heads
+    for r in range(requests):
+        source_pair = r * KVH + own_kv
+        plane = source_pair // pair_dev
+        other = plane != z
+        greeted = greeted + 2 * pieces * other.astype(jnp.int32)
+        for a in range(2):
+            source = (a * pair_dev + source_pair % pair_dev) * per_block + base_piece
+            for piece in range(pieces):
+
+                @pl.when(other)
+                def _(source=source + piece, plane=plane):
+                    pl.semaphore_signal(
+                        barrier,
+                        inc=1,
+                        device_id={"seq": source, "head": plane},
+                        device_id_type=MESH,
+                    )
 
     for copy in loads[:3]:
         copy.wait()
-    own_block = me // per_block
-    own_piece = me % per_block
+    loads[-1].start()
     owned = me * blocks_dev + lax.broadcasted_iota(jnp.int32, (blocks_dev, 1), 0)
 
     sends = []
@@ -137,7 +170,7 @@
             stat_out[step, piece, 0:1, :] = peak[:, columns]
             stat_out[step, piece, 1:2, :] = total[:, columns]
         if step == blocks - 1:
-            pl.semaphore_wait(barrier, seq_n + head_n - 2)
+            pl.semaphore_wait(barrier, greeted)
         for j in range(per_block):
             k = step * per_block + j
             if k == 0:
@@ -162,9 +195,7 @@
 
     for copy in loads[4:8]:
         copy.wait()
-    own_attention = own_block // pair_dev
-    own_pair = own_block % pair_dev
-    request = (z * pair_dev + own_pair) // KVH
+    request = own_whole // KVH
     own_rows = q_v[own_block, pl.ds(pl.multiple_of(own_piece * chunk, chunk), chunk), :]
     tree_scores = contract(tk_ref[own_block], own_rows, 1, 1)
     allowed = contract(anc_ref[request].astype(F32).astype(BF16), spread_ref[...], 0, 0)
@@ -187,56 +218,38 @@
     summed = tree_sum * factors[0] + acc_out[0, own_piece].astype(F32) * factors[1]
     for k in range(1, seq_n):
         summed = summed + acc_in[k].astype(F32) * factors[k + 1]
-    zbuf[0] = jnp.transpose(summed / total).astype(BF16)
+    done_rows[...] = jnp.transpose(summed / total).astype(BF16)
 
     hops = []
-    for k in range(1, head_n):
-        copy = pltpu.make_async_remote_copy(
-            src_ref=zbuf.at[0],
-            dst_ref=zbuf.at[k],
+    for k in reversed(range(head_n)):
+        remote = pltpu.make_async_remote_copy(
+            src_ref=done_rows,
+            dst_ref=parts.at[slot],
             send_sem=s2.at[k],
-            recv_sem=r2.at[k],
-            device_id={"head": flip(z, k)},
+            recv_sem=r2.at[slot],
+            device_id={"seq": holder, "head": flip(z, k)},
             device_id_type=MESH,
         )
-        copy.start()
-        hops.append(copy)
-    routes = []
-    for k in range(head_n):
         if k > 0:
-            hops[k - 1].wait_recv()
-        origin = flip(z, k)
-        whole_pair = origin * pair_dev + own_pair
-        first_head = (whole_pair % KVH) * groups + own_piece * chunk_heads
-        target = first_head // heads_dev
-        slot = (own_attention * requests + whole_pair // KVH) * pieces + (
-            first_head % heads_dev
-        ) // chunk_heads
-
-        remote = pltpu.make_async_remote_copy(
-            src_ref=zbuf.at[k],
-            dst_ref=parts.at[slot],
-            send_sem=s3.at[k],
-            recv_sem=r3.at[slot],
-            device_id={"seq": target},
-            device_id_type=MESH,
-        )
-        here = pltpu.make_async_copy(zbuf.at[k], parts.at[slot], r3.at[slot])
-
-        @pl.when(target != me)
+            remote.start()
+            hops.append(remote)
+            continue
+        here = pltpu.make_async_copy(done_rows, parts.at[slot], r2.at[slot])
+
+        @pl.when(holder != me)
         def _():
             remote.start()
 
-        @pl.when(target == me)
+        @pl.when(holder == me)
         def _():
             here.start()
 
-        routes.append((target, remote))
+        near = remote
 
     for copy in loads[8:]:
         copy.wait()
     for slot in range(2 * requests * pieces):
-        pltpu.make_async_copy(zbuf.at[0], parts.at[slot], r3.at[slot]).wait()
+        pltpu.make_async_copy(done_rows, parts.at[slot], r2.at[slot]).wait()
     stacked = jnp.concatenate(
         [
             jnp.concatenate(
@@ -286,11 +299,10 @@
         copy.wait_send()
     for copy in hops:
         copy.wait_send()
-    for target, remote in routes:
-
-        @pl.when(target != me)
-        def _():
-            remote.wait_send()
+
+    @pl.when(holder != me)
+    def _():
+        near.wait_send()
 
     for _, copy in last:
         copy.wait_send()
@@ -311,7 +323,7 @@
     rows = groups * nodes
     chunk = rows // per_block
     node_dev = nodes // seq_n
-    halves = 2
+    halves = 1
     width = columns // halves
     out_rows = 2 * node_dev * requests
     all_rows = 2 * requests * nodes
@@ -351,7 +363,7 @@
             pltpu.VMEM((blocks, per_block, 8, chunk), F32),
             pltpu.VMEM((seq_n, hd, chunk), BF16),
             pltpu.VMEM((seq_n, 8, chunk), F32),
-            pltpu.VMEM((head_n, chunk, hd), BF16),
+            pltpu.VMEM((chunk, hd), BF16),
             pltpu.VMEM((slots, chunk, hd), BF16),
             pltpu.VMEM((halves, seq_n, out_rows, width), BF16),
             pltpu.VMEM((halves, seq_n, out_rows, width), BF16),
@@ -360,8 +372,6 @@
             dma((seq_n,)),
             dma((seq_n,)),
             dma((seq_n,)),
-            dma((head_n,)),
-            dma((head_n,)),
             dma((head_n,)),
             dma((slots,)),
             dma((halves, seq_n)),

time: 29.7 us -> 25.5 us (0.86)
  Pallas kernels: 27.4 us -> 23.2 us
    pallas_call x1, Pallas kernels: 27.4 us -> 23.2 us  [local(): pl.pallas_call(functools.partial(kernel, dims), out_shape=shape, in_specs...]
where the time goes in v3:
time: 25.5 us; the launch traced here: 25.3 us
  Pallas kernels  23.2 us (91%)
  local copies, waits for them, and re-layouts  1.46 us (6%)
  between operations  0.64 us (3%)
    pallas_call x1, Pallas kernels, local(): pl.pallas_call(functools.partial(kernel, dims), out_shape=shape, in_specs...  23.2 us
    squeeze x1, local copies, waits for them, and re-layouts, local(): return (mixed[0], mixed[1])  1.46 us

profile of v3, /device:TPU:0, one launch (start us, length us, event | category | flops | bytes accessed | tf_op | source)
XLA Modules:
  0.0 25.3 jit_solution(12199176004985927359)
XLA Ops:
  0.6 23.2 %tree_attention.1 = bf16[8,2048]{1,0:T(8,128)(2,1)} custom-call(s32[2,1,32]{2,1,0:T(1,128)} %bitcast.13, s32[1,32,32]{2,1,0:T(8,128)} %anc_hbm.1, bf16[32,128]{1,0:T(8,128)(2,1)} %constant.4.clone.spread_hbm, bf16[64,64]{1,0:T(8,128)(2,1)} %constant.5.clone.order_hbm, bf16[4,32,128]{2,1,0:T(8,128)(2,1)} %bitcast.11, bf16[4,32,128]{2,1,0:T(8,128)(2,1)} %bitcast.12, ...), custom_call_target="tpu_custom_call" | custom-call | tf_op jit(solution)/shard_map/tree_attention/pallas_call | solution.py:346
  23.8 1.5 %slice_bitcast_fusion = (bf16[4,1,2048]{2,0,1:T(4,128)(2,1)}, bf16[4,1,2048]{2,0,1:T(4,128)(2,1)}) fusion(bf16[8,2048]{1,0:T(8,128)(2,1)} %tree_attention.1), kind=kLoop, calls=%fused_computation | loop fusion | bytes 65536 | tf_op jit(solution)/shard_map/squeeze | solution.py:398
